TPU v7x, 512 devices: a whole 4x4x16 slice. The times are simulated.
512 devices in a mesh: outer: 32 (over y, x, core), inner: 16 (over z).
Axes of the slice: x: 4, y: 4, z: 16, core: 2. Of those that a mesh axis runs over, the one named last changes fastest.
Arguments:
- queries: bfloat16 [65536, 2048], P(('outer', 'inner')), may hold values from -6 to 6
- keys: bfloat16 [65536, 2048], P(('outer', 'inner')), may hold values from -6 to 6
- values: bfloat16 [65536, 2048], P(('outer', 'inner')), may hold values from -7 to 7
- cotangent: bfloat16 [65536, 2048], P(('outer', 'inner')), may hold values from -7 to 7
Outputs:
- attended: bfloat16 [65536, 2048], P(('outer', 'inner'))
- query_grad: bfloat16 [65536, 2048], P(('outer', 'inner'))
- key_grad: bfloat16 [65536, 2048], P(('outer', 'inner'))
- value_grad: bfloat16 [65536, 2048], P(('outer', 'inner'))
All inputs are finite; a program needn't handle non-finite values.
Results may differ from a plain program's by a relative error of at most 0.013.
The roundings to bfloat16 on the way count: a program that leaves them out, or rounds other values in their place, can miss the bound.
Values sent between devices are 32-bit elements; how exact they have to be, the bound alone decides.
A program may use at most 128 MiB of HBM per device.

v0:
```python
import jax
import jax.numpy as jnp
from jax import lax
from jax.sharding import PartitionSpec as P

HEADS = 16
HD = 128


def entering(shard, axis, combine, identity, reverse):
    devices, place = (lax.axis_size(axis), lax.axis_index(axis))
    everything = jax.tree.map(lambda part: lax.all_gather(part, axis), shard)
    start = jax.tree.map(
        lambda part, zero: jnp.broadcast_to(jnp.asarray(zero, part.dtype), part.shape),
        shard,
        identity,
    )

    def lap(k, before):
        at = devices - 1 - k if reverse else k
        reached = at > place if reverse else at < place
        new = combine(before, jax.tree.map(lambda part: part[at], everything))
        return jax.tree.map(lambda a, b: jnp.where(reached, a, b), new, before)

    return lax.fori_loop(0, devices, lap, start)


def features(x):
    wide = x.astype(jnp.float32)
    return jnp.where(wide > 0, wide + 1.0, jnp.exp(jnp.minimum(wide, 0.0)))


def slope(x):
    wide = x.astype(jnp.float32)
    return jnp.where(wide > 0, 1.0, jnp.exp(jnp.minimum(wide, 0.0)))


def add_pair(first, second):
    return (first[0] + second[0], first[1] + second[1])


def zero_pair(parts):
    return (jnp.zeros_like(parts[0]), jnp.zeros_like(parts[1]))


def carry_states(parts, backward):
    within = entering(parts, "inner", add_pair, zero_pair(parts), backward)
    shares = (
        lax.psum_scatter(parts[0], "inner", scatter_dimension=0, tiled=True),
        lax.psum_scatter(parts[1], "inner", scatter_dimension=0, tiled=True),
    )
    before = entering(shares, "outer", add_pair, zero_pair(shares), backward)
    spread = (
        lax.all_gather(before[0], "inner", axis=0, tiled=True),
        lax.all_gather(before[1], "inner", axis=0, tiled=True),
    )
    return add_pair(within, spread)


def per_device(queries, keys, values, cotangent):
    count_rows = queries.shape[0]
    shaped = (count_rows, HEADS, HD)
    query_rows = queries.reshape(shaped)
    key_rows = keys.reshape(shaped)
    value_rows = values.reshape(shaped)
    cotan_rows = cotangent.reshape(shaped)
    highest = lax.Precision.HIGHEST
    f32 = jnp.float32
    rows = lax.broadcasted_iota(jnp.int32, (count_rows, count_rows), 0)
    cols = lax.broadcasted_iota(jnp.int32, (count_rows, count_rows), 1)
    causal = (cols <= rows)[None]
    q_feat = features(query_rows).astype(jnp.bfloat16)
    k_feat = features(key_rows).astype(jnp.bfloat16)
    q_wide = q_feat.astype(f32)
    scores = jnp.einsum("thd,shd->hts", q_feat, k_feat, preferred_element_type=f32)
    scores = jnp.where(causal, scores, 0.0)
    weights = scores.astype(jnp.bfloat16)
    local_state = jnp.einsum("shd,she->hde", k_feat, value_rows, preferred_element_type=f32)
    local_norm = jnp.sum(k_feat.astype(f32), axis=0)
    intra_num = jnp.einsum("hts,she->the", weights, value_rows, preferred_element_type=f32)
    intra_den = jnp.sum(scores, axis=2).T
    state, normal = carry_states((local_state, local_norm), False)
    state_low = state.astype(jnp.bfloat16)
    den = intra_den + jnp.einsum("thd,hd->th", q_wide, normal, precision=highest)
    num = intra_num + jnp.einsum("thd,hde->the", q_feat, state_low, preferred_element_type=f32)
    ratio = num / den[:, :, None]
    attended = ratio.astype(jnp.bfloat16)
    cotan_wide = cotan_rows.astype(f32)
    grad_scaled = (cotan_wide / den[:, :, None]).astype(jnp.bfloat16)
    grad_den = -jnp.sum(cotan_wide * ratio, axis=2) / den
    grad_scores = jnp.einsum("the,she->hts", grad_scaled, value_rows, preferred_element_type=f32)
    grad_scores = jnp.where(causal, grad_scores + grad_den.T[:, :, None], 0.0).astype(jnp.bfloat16)
    later_local = jnp.einsum("thd,the->hde", q_feat, grad_scaled, preferred_element_type=f32)
    later_norm_local = jnp.einsum("th,thd->hd", grad_den, q_wide, precision=highest)
    q_lin = jnp.einsum("hts,shd->thd", grad_scores, k_feat, preferred_element_type=f32)
    q_lin = q_lin + jnp.einsum("the,hde->thd", grad_scaled, state_low, preferred_element_type=f32)
    q_lin = q_lin + grad_den[:, :, None] * normal[None]
    query_grad = (q_lin * slope(query_rows)).astype(jnp.bfloat16)
    k_intra = jnp.einsum("hts,thd->shd", grad_scores, q_feat, preferred_element_type=f32)
    v_intra = jnp.einsum("hts,the->she", weights, grad_scaled, preferred_element_type=f32)
    later, later_norm = carry_states((later_local, later_norm_local), True)
    later_low = later.astype(jnp.bfloat16)
    k_lin = k_intra + jnp.einsum("she,hde->shd", value_rows, later_low, preferred_element_type=f32)
    k_lin = k_lin + later_norm[None]
    key_grad = (k_lin * slope(key_rows)).astype(jnp.bfloat16)
    value_grad = v_intra + jnp.einsum("shd,hde->she", k_feat, later_low, preferred_element_type=f32)
    flat = (count_rows, HEADS * HD)
    return (
        attended.reshape(flat),
        query_grad.reshape(flat),
        key_grad.reshape(flat),
        value_grad.astype(jnp.bfloat16).reshape(flat),
    )


def solution(mesh):
    placed = (
        P(("outer", "inner"), None),
        P(("outer", "inner"), None),
        P(("outer", "inner"), None),
        P(("outer", "inner"), None),
    )
    return jax.shard_map(
        per_device,
        mesh=mesh,
        in_specs=placed,
        out_specs=(
            P(("outer", "inner"), None),
            P(("outer", "inner"), None),
            P(("outer", "inner"), None),
            P(("outer", "inner"), None),
        ),
        check_vma=False,
    )
```

profile of v0, /device:TPU:1, one launch (start us, length us, event | category | flops | bytes accessed | tf_op | source)
XLA Modules:
  0.0 835.8 jit_solution(9513338945042740394)
XLA Ops:
  7.2 2.5 fusion.20
  11.6 66.5 %reduce-scatter.3.cloned.1.call-done = f32[1,128,128]{2,1,0:T(8,128)} async-done(((f32[16,128,128]{2,1,0:T(8,128)}), f32[1,128,128]{2,1,0:T(8,128)}) %reduce-scatter.3.cloned.1.call-update) | async-done | bytes 65552 | tf_op jit(solution)/shard_map/reduce_scatter | solution.py:49
  79.0 2.2 copy.48
  81.2 2.4 fusion.16
  87.4 22.0 %all-reduce = f32[16,128]{1,0:T(8,128)S(1)} all-reduce(f32[16,128]{1,0:T(8,128)S(1)} %bitcast.183), channel_id=10, replica_groups=mesh['outer'=32,'inner'=16] {'inner'}, use_global_device_ids=true, to_apply=%region_4.5.clone | all-reduce | flops 2048 | bytes 16384
  110.1 39.2 %all-gather.7 = f32[32,1,128]{2,1,0:T(1,128)S(1)} all-gather(f32[1,1,128]{2,1,0:T(1,128)S(1)} %fusion.46), channel_id=4, replica_groups=mesh['outer'=32,'inner'=16] {'outer'}, dimensions={0}, use_global_device_ids=true | all-gather | bytes 16896 | tf_op jit(solution)/shard_map/all_gather | solution.py:12
  149.3 21.6 %all_gather.63 = f32[16,16,128]{2,1,0:T(8,128)S(1)} all-gather(f32[1,16,128]{2,1,0:T(8,128)S(1)} %bitcast.184), channel_id=1, replica_groups=mesh['outer'=32,'inner'=16] {'inner'}, dimensions={0}, use_global_device_ids=true | all-gather | bytes 139264 | tf_op jit(solution)/shard_map/all_gather | solution.py:12
  172.2 28.9 %while.69 = (s32[]{:T(128)}, f32[1,128,128]{2,1,0:T(8,128)S(1)}, f32[1,128]{1,0:T(1,128)S(1)}, s32[]{:T(128)}, f32[32,1,128,128]{3,2,1,0:T(8,128)}, /*index=5*/f32[32,1,128]{2,1,0:T(1,128)S(1)}, s32[]{:T(128)}, s32[]{:T(128)}) while((s32[]{:T(128)}, f32[1,128,128]{2,1,0:T(8,128)S(1)}, f32[1,128]{1,0:T(1,128)S(1)}, s32[]{:T(128)}, ...), condition=%wide.region_6.7_spmd.clone, body=%wide.region_5.6_spmd.clone.sunk | while | flops 49540 | bytes 198267 | solution.py:25
  201.1 24.5 %all-gather.8 = f32[16,1,128]{2,1,0:T(1,128)S(1)} all-gather(f32[1,1,128]{2,1,0:T(1,128)S(1)} %bitcast.193), channel_id=1, replica_groups=mesh['outer'=32,'inner'=16] {'inner'}, dimensions={0}, use_global_device_ids=true | all-gather | bytes 8704 | tf_op jit(solution)/shard_map/all_gather | solution.py:55
  225.7 114.5 %all-gather.22.cloned.1.call-done = f32[256,128,128]{2,1,0:T(8,128)} async-done(((f32[16,128,128]{2,1,0:T(8,128)}), f32[256,128,128]{2,1,0:T(8,128)}) %all-gather.22.cloned.1.call-update) | async-done | bytes 16777232 | tf_op jit(solution)/shard_map/all_gather | solution.py:12
  340.2 26.1 %while.68 = (s32[]{:T(128)}, f32[16,128,128]{2,1,0:T(8,128)S(1)}, f32[16,128]{1,0:T(8,128)S(1)}, s32[]{:T(128)}, f32[16,16,128,128]{3,2,1,0:T(8,128)}, /*index=5*/f32[16,16,128]{2,1,0:T(8,128)S(1)}, s32[]{:T(128)}, s32[]{:T(128)}) while((s32[]{:T(128)}, f32[16,128,128]{2,1,0:T(8,128)S(1)}, f32[16,128]{1,0:T(8,128)S(1)}, s32[]{:T(128)}, ...), condition=%wide.region_2.3_spmd.clone, body=%wide.region_1.2_spmd.clone.sunk | while | flops 792580 | bytes 3170427 | solution.py:25
  370.3 58.2 %reduce-scatter.5.cloned.1.call-done = f32[1,128,128]{2,1,0:T(8,128)} async-done(((f32[16,128,128]{2,1,0:T(8,128)}), f32[1,128,128]{2,1,0:T(8,128)}) %reduce-scatter.5.cloned.1.call-update) | async-done | bytes 65552 | tf_op jit(solution)/shard_map/reduce_scatter | solution.py:49
  429.4 2.5 copy.55
  432.0 2.5 copy.62
  434.5 64.9 %all-gather.18.cloned.1.call-done = f32[16,128,128]{2,1,0:T(8,128)} async-done(((f32[1,128,128]{2,1,0:T(8,128)}), f32[16,128,128]{2,1,0:T(8,128)}) %all-gather.18.cloned.1.call-update) | async-done | bytes 1048592 | tf_op jit(solution)/shard_map/all_gather | solution.py:54
  501.5 1.6 convolution_bitcast_fusion.1
  503.2 2.6 multiply_reduce_fusion
  505.8 2.0 copy.66
  510.2 2.6 fusion.10
  512.8 2.0 copy.67
  515.4 23.2 %all-reduce.1 = f32[16,128]{1,0:T(8,128)S(1)} all-reduce(f32[16,128]{1,0:T(8,128)S(1)} %bitcast.185), channel_id=12, replica_groups=mesh['outer'=32,'inner'=16] {'inner'}, use_global_device_ids=true, to_apply=%region_12.13.clone | all-reduce | flops 2048 | bytes 16384
  539.2 39.7 %all-gather.9 = f32[32,1,128]{2,1,0:T(1,128)S(1)} all-gather(f32[1,1,128]{2,1,0:T(1,128)S(1)} %fusion.47), channel_id=8, replica_groups=mesh['outer'=32,'inner'=16] {'outer'}, dimensions={0}, use_global_device_ids=true | all-gather | bytes 16896 | tf_op jit(solution)/shard_map/all_gather | solution.py:12
  578.9 22.4 %all-gather.4 = f32[256,128]{1,0:T(8,128)S(1)} all-gather(f32[16,128]{1,0:T(8,128)S(1)} %bitcast.186), channel_id=6, replica_groups=mesh['outer'=32,'inner'=16] {'inner'}, dimensions={0}, use_global_device_ids=true | all-gather | bytes 139264 | tf_op jit(solution)/shard_map/all_gather | solution.py:12
  601.3 2.5 fusion.53
  603.8 2.5 fusion.41
  606.3 29.1 %while.71 = (s32[]{:T(128)}, f32[1,128,128]{2,1,0:T(8,128)S(1)}, f32[1,128]{1,0:T(1,128)S(1)}, s32[]{:T(128)}, f32[32,1,128,128]{3,2,1,0:T(8,128)}, /*index=5*/f...) while((s32[]{:T(128)}, f32[1,128,128]{2,1,0:T(8,128)S(1)}, ...), condition=%wide.region_14.15_spmd.clone, body=%wide.region_13.14_spmd.clone.sunk | while | flops 49544 | bytes 198329 | solution.py:25
  635.5 25.2 %all-gather.10 = f32[16,1,128]{2,1,0:T(1,128)S(1)} all-gather(f32[1,1,128]{2,1,0:T(1,128)S(1)} %bitcast.192), channel_id=1, replica_groups=mesh['outer'=32,'inner'=16] {'inner'}, dimensions={0}, use_global_device_ids=true | all-gather | bytes 8704 | tf_op jit(solution)/shard_map/all_gather | solution.py:55
  660.7 100.4 %all-gather.26.cloned.1.call-done = f32[256,128,128]{2,1,0:T(8,128)} async-done(((f32[16,128,128]{2,1,0:T(8,128)}), f32[256,128,128]{2,1,0:T(8,128)}) %all-gather.26.cloned.1.call-update) | async-done | bytes 16777232 | tf_op jit(solution)/shard_map/all_gather | solution.py:12
  761.1 26.3 %while.70 = (s32[]{:T(128)}, f32[16,128,128]{2,1,0:T(8,128)S(1)}, f32[16,128]{1,0:T(8,128)S(1)}, s32[]{:T(128)}, f32[16,16,128,128]{3,2,1,0:T(8,128)}, /*index=5...) while((s32[]{:T(128)}, f32[16,128,128]{2,1,0:T(8,128)S(1)}, ...), condition=%wide.region_10.11_spmd.clone, body=%wide.region_9.10_spmd.clone.sunk | while | flops 792584 | bytes 3170489 | solution.py:25
  787.3 34.5 %all-gather.20.cloned.1.call-done = f32[16,128,128]{2,1,0:T(8,128)} async-done(((f32[1,128,128]{2,1,0:T(8,128)}), f32[16,128,128]{2,1,0:T(8,128)}) %all-gather.20.cloned.1.call-update) | async-done | bytes 1048592 | tf_op jit(solution)/shard_map/all_gather | solution.py:54
  823.2 2.0 fusion.11
  826.2 1.7 fusion.12
  (267 shorter events, 129.8 us)
Async XLA Ops:
  7.2 3.1 copy-start
  7.2 70.9 %reduce-scatter.3.cloned.1.call-start = ((), (), s32[]{:S(2)}) async-start(), calls=%async_computation.2 | async-start | bytes 1114112 | tf_op jit(solution)/shard_map/reduce_scatter | solution.py:49
  9.7 357.2 %copy-start.9 = (bf16[16,16,8,128]{3,2,1,0:T(8,128)(2,1)}, bf16[16,16,8,128]{3,2,1,0:T(8,128)(2,1)S(1)}, u32[]{:S(2)}) copy-start(bf16[16,16,8,128]{3,2,1,0:T(8,128)(2,1)S(1)} %get-tuple-element.710) | copy-start | bytes 1572868
  10.3 68.6 %copy-start.6 = (bf16[128,16,128]{0,2,1:T(8,128)(2,1)}, bf16[128,16,128]{0,2,1:T(8,128)(2,1)S(1)}, u32[]{:S(2)}) copy-start(bf16[128,16,128]{0,2,1:T(8,128)(2,1)S(1)} %copy.43) | copy-start | bytes 1572868
  11.6 160.6 %all-gather.24.cloned.1.call-start = ((), (), s32[]{:S(2)}) async-start(), calls=%async_computation.7 | async-start | bytes 2162688 | tf_op jit(solution)/shard_map/all_gather | solution.py:12
  78.1 262.0 %all-gather.22.cloned.1.call-start = ((), (), s32[]{:S(2)}) async-start(), calls=%async_computation.6 | async-start | bytes 17825792 | tf_op jit(solution)/shard_map/all_gather | solution.py:12
  78.9 349.7 %reduce-scatter.5.cloned.1.call-start = ((), (), s32[]{:S(2)}) async-start(), calls=%async_computation.4 | async-start | bytes 1114112 | tf_op jit(solution)/shard_map/reduce_scatter | solution.py:49
  83.6 345.8 %copy-start.4 = (bf16[16,16,8,128]{3,2,1,0:T(8,128)(2,1)}, bf16[16,16,8,128]{3,2,1,0:T(8,128)(2,1)S(1)}, u32[]{:S(2)}) copy-start(bf16[16,16,8,128]{3,2,1,0:T(8,128)(2,1)S(1)} %get-tuple-element.713) | copy-start | bytes 1572868
  86.0 343.3 %copy-start.1 = (bf16[128,16,128]{0,2,1:T(8,128)(2,1)}, bf16[128,16,128]{0,2,1:T(8,128)(2,1)S(1)}, u32[]{:S(2)}) copy-start(bf16[128,16,128]{0,2,1:T(8,128)(2,1)S(1)} %copy.56) | copy-start | bytes 1572868
  201.1 168.6 %copy-start.8 = (f32[1,128,128]{2,1,0:T(8,128)}, f32[1,128,128]{2,1,0:T(8,128)S(1)}, u32[]{:S(2)}) copy-start(f32[1,128,128]{2,1,0:T(8,128)S(1)} %get-tuple-element.535) | copy-start | bytes 196612
  369.7 129.7 %all-gather.18.cloned.1.call-start = ((), (), s32[]{:S(2)}) async-start(), calls=%async_computation.3 | async-start | bytes 1114112 | tf_op jit(solution)/shard_map/all_gather | solution.py:54
  370.3 236.1 %all-gather.28.cloned.1.call-start = ((), (), s32[]{:S(2)}) async-start(), calls=%async_computation.9 | async-start | bytes 2162688 | tf_op jit(solution)/shard_map/all_gather | solution.py:12
  428.6 332.5 %all-gather.26.cloned.1.call-start = ((), (), s32[]{:S(2)}) async-start(), calls=%async_computation.8 | async-start | bytes 17825792 | tf_op jit(solution)/shard_map/all_gather | solution.py:12
  429.3 392.5 %all-gather.20.cloned.1.call-start = ((), (), s32[]{:S(2)}) async-start(), calls=%async_computation.5 | async-start | bytes 1114112 | tf_op jit(solution)/shard_map/all_gather | solution.py:54
  500.7 0.8 copy-start.3
  501.5 13.4 %copy-start.5 = (bf16[16,16,8,128]{3,2,1,0:T(8,128)(2,1)S(1)}, bf16[16,16,8,128]{3,2,1,0:T(8,128)(2,1)}, u32[]{:S(2)}) copy-start(bf16[16,16,8,128]{3,2,1,0:T(8,128)(2,1)} %copy-done.4) | copy-start | bytes 1572868
  501.5 99.8 %copy-start.2 = (bf16[128,16,128]{0,2,1:T(8,128)(2,1)S(1)}, bf16[128,16,128]{0,2,1:T(8,128)(2,1)}, u32[]{:S(2)}) copy-start(bf16[128,16,128]{0,2,1:T(8,128)(2,1)} %copy-done.1) | copy-start | bytes 1572868
  508.1 0.8 copy-start.11
  515.4 310.8 %copy-start.10 = (bf16[16,16,8,128]{3,2,1,0:T(8,128)(2,1)S(1)}, bf16[16,16,8,128]{3,2,1,0:T(8,128)(2,1)}, u32[]{:S(2)}) copy-start(bf16[16,16,8,128]{3,2,1,0:T(8,128)(2,1)} %copy-done.9) | copy-start | bytes 1572868
  635.4 25.2 %copy-start.7 = (f32[1,128,128]{2,1,0:T(8,128)}, f32[1,128,128]{2,1,0:T(8,128)S(1)}, u32[]{:S(2)}) copy-start(f32[1,128,128]{2,1,0:T(8,128)S(1)} %get-tuple-element.539) | copy-start | bytes 196612
Sparse Core Ops, SparseCore 0:
  11.7 66.3 reduce-scatter.2
  81.3 67.1 all-gather.23
  150.6 189.5 all-gather.21
  369.8 58.6 reduce-scatter.4
  431.0 68.2 all-gather.17
  502.4 66.5 all-gather.27
  571.1 189.9 all-gather.25
  763.7 58.0 all-gather.19
where the time goes:
time: 851 us; the launch traced here: 836 us
  waiting for transfers between devices  441 us (52%)
  blocking collectives  218 us (26%)
  other arithmetic  116 us (14%)
  matrix products  22.3 us (3%)
  local copies, waits for them, and re-layouts  20.7 us (2%)
  between operations  14.5 us (2%)
    all_gather x4, waiting for transfers between devices, entering(): everything = jax.tree.map(lambda part: lax.all_gather(part, axis), shard)  215 us
    reduce_scatter x2, waiting for transfers between devices, carry_states(): lax.psum_scatter(parts[0], 'inner', scatter_dimension=0, tiled=True)  125 us
    all_gather x4, blocking collectives, entering(): everything = jax.tree.map(lambda part: lax.all_gather(part, axis), shard)  123 us
    select_n x192, other arithmetic, lap(): return jax.tree.map(lambda a, b: jnp.where(reached, a, b), new, before)  107 us
    all_gather x2, waiting for transfers between devices, carry_states(): lax.all_gather(before[0], 'inner', axis=0, tiled=True)  99.4 us
    all_gather x2, blocking collectives, carry_states(): lax.all_gather(before[1], 'inner', axis=0, tiled=True)  49.7 us
    unnamed x2, blocking collectives  45.2 us
  transfers between devices with their start and end apart: 8, of which 6 were waited for; matrix products, arithmetic and copies ran while one was open for 14% of the time, Pallas kernels for 0%

commit v1 on v0

--- a/solution.py
+++ b/solution.py
@@ -1,28 +1,249 @@
+import functools
+
 import jax
 import jax.numpy as jnp
 from jax import lax
+from jax.experimental import pallas as pl
+from jax.experimental.pallas import tpu as pltpu
 from jax.sharding import PartitionSpec as P
 
 HEADS = 16
 HD = 128
-
-
-def entering(shard, axis, combine, identity, reverse):
-    devices, place = (lax.axis_size(axis), lax.axis_index(axis))
-    everything = jax.tree.map(lambda part: lax.all_gather(part, axis), shard)
-    start = jax.tree.map(
-        lambda part, zero: jnp.broadcast_to(jnp.asarray(zero, part.dtype), part.shape),
-        shard,
-        identity,
-    )
-
-    def lap(k, before):
-        at = devices - 1 - k if reverse else k
-        reached = at > place if reverse else at < place
-        new = combine(before, jax.tree.map(lambda part: part[at], everything))
-        return jax.tree.map(lambda a, b: jnp.where(reached, a, b), new, before)
-
-    return lax.fori_loop(0, devices, lap, start)
+MESH = pl.DeviceIdType.MESH
+NZ, NX, NY = 16, 4, 4
+R = 1088
+
+
+def scan_kernel(rev, rz, rp, n, s_ref, p_ref, oth, uin, uout, din, dout, yin, yout, xpin, xpout, xmin, xmout, pin, pout, rs, ss):
+    rows = R // n
+    z = lax.axis_index("inner")
+    outer = lax.axis_index("outer")
+    core = lax.rem(outer, 2)
+    x = lax.rem(outer // 2, NX)
+    y = outer // (2 * NX)
+    flip = (lambda v, m: m - 1 - v) if rev else (lambda v, m: v)
+    zc, xc, yc, cc = flip(z, NZ), flip(x, NX), flip(y, NY), flip(core, 2)
+
+    def dev(y_, x_, c_, z_):
+        return {"outer": (y_ * NX + x_) * 2 + c_, "inner": z_}
+
+    step = -1 if rev else 1
+    zn = lax.rem(z + step + NZ, NZ)
+    zp = lax.rem(z - step + NZ, NZ)
+    xn = lax.rem(x + step + NX, NX)
+    xp = lax.rem(x - step + NX, NX)
+    yn = lax.rem(y + step + NY, NY)
+    yp = lax.rem(y - step + NY, NY)
+    d_zn, d_zp = dev(y, x, core, zn), dev(y, x, core, zp)
+    d_xn, d_xp = dev(y, xn, core, z), dev(y, xp, core, z)
+    d_yn, d_yp = dev(yn, x, core, z), dev(yp, x, core, z)
+    d_oc = dev(y, x, 1 - core, z)
+
+    bar = pltpu.get_barrier_semaphore()
+    for d in (d_zn, d_zp, d_xn, d_xp, d_yn, d_yp, d_oc):
+        pl.semaphore_signal(bar, inc=1, device_id=d, device_id_type=MESH)
+
+    @pl.when(zc == 0)
+    def _():
+        uin[...] = jnp.zeros_like(uin)
+
+    @pl.when(zc == NZ - 1)
+    def _():
+        din[...] = jnp.zeros_like(din)
+
+    @pl.when(yc == 0)
+    def _():
+        yin[...] = jnp.zeros_like(yin)
+
+    @pl.when(xc == 0)
+    def _():
+        xpin[...] = jnp.zeros_like(xpin)
+
+    @pl.when(xc == NX - 1)
+    def _():
+        xmin[...] = jnp.zeros_like(xmin)
+
+    pl.semaphore_wait(bar, 7)
+
+    def rc(k, src, dst, d, i):
+        return pltpu.make_async_remote_copy(src_ref=src, dst_ref=dst, send_sem=ss.at[k], recv_sem=rs.at[k, i], device_id=d, device_id_type=MESH)
+
+    def cut(i):
+        return pl.ds(pl.multiple_of(i * rows, 8), rows)
+
+    def ex(i):
+        return rc(0, s_ref.at[1 - core, cut(i)], oth.at[cut(i)], d_oc, i)
+
+    def up(i):
+        return rc(1, uout.at[i], uin.at[i], d_zn, i)
+
+    def down(i):
+        return rc(2, dout.at[i], din.at[i], d_zp, i)
+
+    def yy(i):
+        return rc(3, yout.at[i], yin.at[i], d_yn, i)
+
+    def xpl(i):
+        return rc(4, xpout.at[i], xpin.at[i], d_xn, i)
+
+    def xmi(i):
+        return rc(5, xmout.at[i], xmin.at[i], d_xp, i)
+
+    def px(i):
+        return rc(6, pout.at[i], pin.at[i], d_oc, i)
+
+    @pl.loop(0, n)
+    def _(i):
+        ex(i).start()
+
+    oU = rz * zc
+    oD = rz * (NZ - 1 - zc)
+    oY = jnp.maximum(oU, oD) + rp * yc
+    oXp = oY + rp * xc
+    oXm = oY + rp * (NX - 1 - xc)
+    oF = jnp.maximum(oXp, oXm)
+    first = jnp.minimum(oU, oD)
+
+    def ac(i):
+        own = s_ref[core, cut(i)]
+        other = oth[cut(i)]
+        return jnp.where(cc == 0, own, other), own + other
+
+    def on(i, f):
+        @pl.when(jnp.logical_and(i >= 0, i < n))
+        def _():
+            f(i)
+
+    def sU(i):
+        @pl.when(zc > 0)
+        def _():
+            up(i).wait_recv()
+
+        a, c = ac(i)
+        uout[i, 0] = uin[i, 0] + a
+        uout[i, 1] = uin[i, 1] + c
+
+        @pl.when(zc < NZ - 1)
+        def _():
+            up(i).start()
+
+    def sD(i):
+        @pl.when(zc < NZ - 1)
+        def _():
+            down(i).wait_recv()
+
+        a, c = ac(i)
+        dout[i, 0] = din[i, 0] + a
+        dout[i, 1] = din[i, 1] + c
+
+        @pl.when(zc > 0)
+        def _():
+            down(i).start()
+
+    def sY(i):
+        @pl.when(yc > 0)
+        def _():
+            yy(i).wait_recv()
+
+        yout[i] = yin[i] + (uout[i, 1] + din[i, 1])
+
+        @pl.when(yc < NY - 1)
+        def _():
+            yy(i).start()
+
+    def sXp(i):
+        @pl.when(xc > 0)
+        def _():
+            xpl(i).wait_recv()
+
+        xpout[i] = xpin[i] + yout[i]
+
+        @pl.when(xc < NX - 1)
+        def _():
+            xpl(i).start()
+
+    def sXm(i):
+        @pl.when(xc < NX - 1)
+        def _():
+            xmi(i).wait_recv()
+
+        xmout[i] = xmin[i] + yin[i]
+
+        @pl.when(xc > 0)
+        def _():
+            xmi(i).start()
+
+    def sF(i):
+        cc_ = xpin[i] + xmout[i]
+        p0 = cc_ + uin[i, 0]
+        p1 = cc_ + uin[i, 1] + dout[i, 0]
+        p_ref[core, cut(i)] = jnp.where(cc == 0, p0, p1)
+        pout[i] = jnp.where(cc == 0, p1, p0)
+        px(i).start()
+
+    def slot(s, carry):
+        def early(i):
+            ex(i).wait_recv()
+
+        on(s - first, early)
+        on(s - oU, sU)
+        on(s - oD, sD)
+        on(s - oY, sY)
+        on(s - oXp, sXp)
+        on(s - oXm, sXm)
+        on(s - oF, sF)
+        return carry
+
+    lax.fori_loop(0, n + rz * (NZ - 1) + rp * (NY - 1 + NX - 1), slot, 0)
+
+    @pl.loop(0, n)
+    def _(i):
+        px(i).wait_recv()
+        p_ref[1 - core, cut(i)] = pin[i]
+
+    def whole(k, buf, d):
+        return pltpu.make_async_remote_copy(src_ref=buf, dst_ref=buf, send_sem=ss.at[k], recv_sem=rs.at[k, 0], device_id=d, device_id_type=MESH)
+
+    whole(0, oth, d_oc).wait_send()
+
+    @pl.when(zc < NZ - 1)
+    def _():
+        whole(1, uout, d_zn).wait_send()
+
+    @pl.when(zc > 0)
+    def _():
+        whole(2, dout, d_zp).wait_send()
+
+    @pl.when(yc < NY - 1)
+    def _():
+        whole(3, yout, d_yn).wait_send()
+
+    @pl.when(xc < NX - 1)
+    def _():
+        whole(4, xpout, d_xn).wait_send()
+
+    @pl.when(xc > 0)
+    def _():
+        whole(5, xmout, d_xp).wait_send()
+
+    whole(6, pout, d_oc).wait_send()
+
+
+def scan(s, rev, n=34, rz=4, rp=4):
+    rows = R // n
+    f32 = jnp.float32
+    one = pltpu.VMEM((n, rows, 128), f32)
+    two = pltpu.VMEM((n, 2, rows, 128), f32)
+    return pl.pallas_call(
+        functools.partial(scan_kernel, rev, rz, rp, n),
+        out_shape=jax.ShapeDtypeStruct((2, R, 128), f32),
+        in_specs=[pl.BlockSpec(memory_space=pltpu.VMEM)],
+        out_specs=pl.BlockSpec(memory_space=pltpu.VMEM),
+        scratch_shapes=[pltpu.VMEM((R, 128), f32), two, two, two, two, one, one, one, one, one, one, one, one,
+                        pltpu.SemaphoreType.DMA((7, n)), pltpu.SemaphoreType.DMA((7,))],
+        compiler_params=pltpu.CompilerParams(collective_id=1 if rev else 0, has_side_effects=True, vmem_limit_bytes=60 << 20),
+        name="scan_rev" if rev else "scan_fwd",
+    )(s)
 
 
 def features(x):
@@ -35,26 +256,16 @@
     return jnp.where(wide > 0, 1.0, jnp.exp(jnp.minimum(wide, 0.0)))
 
 
-def add_pair(first, second):
-    return (first[0] + second[0], first[1] + second[1])
-
-
-def zero_pair(parts):
-    return (jnp.zeros_like(parts[0]), jnp.zeros_like(parts[1]))
-
-
 def carry_states(parts, backward):
-    within = entering(parts, "inner", add_pair, zero_pair(parts), backward)
-    shares = (
-        lax.psum_scatter(parts[0], "inner", scatter_dimension=0, tiled=True),
-        lax.psum_scatter(parts[1], "inner", scatter_dimension=0, tiled=True),
+    state, norm = parts
+    half = HEADS // 2
+    norms = jnp.pad(norm.reshape(2, half, HD), ((0, 0), (0, R - half * HD - half), (0, 0)))
+    both = jnp.concatenate([state.reshape(2, half * HD, HD), norms], axis=1)
+    out = scan(both, backward)
+    return (
+        out[:, : half * HD].reshape(HEADS, HD, HD),
+        out[:, half * HD : half * HD + half].reshape(HEADS, HD),
     )
-    before = entering(shares, "outer", add_pair, zero_pair(shares), backward)
-    spread = (
-        lax.all_gather(before[0], "inner", axis=0, tiled=True),
-        lax.all_gather(before[1], "inner", axis=0, tiled=True),
-    )
-    return add_pair(within, spread)
 
 
 def per_device(queries, keys, values, cotangent):

time: 851 us -> 246 us (0.29); the launches traced: 836 us -> 245 us
  waiting for transfers between devices: 441 us -> 0 us
  blocking collectives: 218 us -> 0 us
  Pallas kernels: 0 us -> 209 us
  other arithmetic: 116 us -> 6.61 us
  between operations: 14.5 us -> 0.82 us
  matrix products: 22.3 us -> 9.83 us
    all_gather x6 -> x0, waiting for transfers between devices: 314 us -> none  [the longest x4 215 us: entering(): everything = jax.tree.map(lambda part: lax.all_gather(part, axis), shard)]
    pallas_call x0 -> x2, Pallas kernels: none -> 209 us  [scan(): pl.pallas_call(functools.partial(scan_kernel, rev, rz, rp, n), out_shape=...]
    all_gather x6 -> x0, blocking collectives: 173 us -> none  [the longest x4 123 us: entering(): everything = jax.tree.map(lambda part: lax.all_gather(part, axis), shard)]
    reduce_scatter x2 -> x0, waiting for transfers between devices: 125 us -> none  [carry_states(): lax.psum_scatter(parts[0], 'inner', scatter_dimension=0, tiled=True)]
    select_n x192 -> x0, other arithmetic: 107 us -> none  [lap(): return jax.tree.map(lambda a, b: jnp.where(reached, a, b), new, before)]
    unnamed x2 -> x0, blocking collectives: 45.2 us -> none
  transfers between devices with their start and end apart: 8 -> 0, of which waited for: 6 -> 0; matrix products, arithmetic and copies ran while one was open for 14% -> 0% of each run, Pallas kernels for 0% -> 0%
where the time goes in v1:
time: 246 us; the launch traced here: 245 us
  Pallas kernels  209 us (85%)
  local copies, waits for them, and re-layouts  19.1 us (8%)
  matrix products  9.83 us (4%)
  other arithmetic  6.61 us (3%)
    pallas_call x2, Pallas kernels, scan(): pl.pallas_call(functools.partial(scan_kernel, rev, rz, rp, n), out_shape=...  209 us
    unnamed x30, local copies, waits for them, and re-layouts  7.94 us

profile of v1, /device:TPU:1, one launch (start us, length us, event | category | flops | bytes accessed | tf_op | source)
XLA Modules:
  0.0 245.1 jit_solution(11587933866427577382)
XLA Ops:
  0.7 2.3 copy.16
  3.0 3.1 %fusion.16 = (f32[128,2048]{1,0:T(8,128)}, bf16[16,16,8,128]{3,2,1,0:T(8,128)(2,1)S(1)}, bf16[16,8,16,128]{3,1,2,0:T(8,128)(2,1)S(1)}, bf16[16,8,16,128]{3,1,2,0...) fusion(bf16[128,2048]{1,0:T(8,128)(2,1)S(1)} %copy-done.9, ...), kind=kLoop, calls=%fused_computation.32 | loop fusion | flops 4192256 | bytes 5251072 | tf_op jit(solution)/shard_map/jit(_where)/select_n | solution.py:256
  6.1 1.3 fusion.48
  7.5 0.5 copy.12
  8.3 1.1 select_maximum_fusion.1.s_ref
  9.4 101.6 %scan_fwd.1 = f32[2,1088,128]{2,1,0:T(8,128)} custom-call(f32[2,1088,128]{2,1,0:T(8,128)} %select_maximum_fusion.1.s_ref), custom_call_target="tpu_custom_call" | custom-call | tf_op jit(solution)/shard_map/scan_fwd/pallas_call | solution.py:237
  111.0 0.7 slice_bitcast_fusion.1
  112.3 0.5 fusion.49
  112.8 1.3 slice.25
  114.1 0.5 convolution_bitcast_fusion.1
  114.6 0.7 copy-done.5
  115.9 1.0 copy.33
  116.9 2.5 %copy.23 = f32[128,2048]{0,1:T(8,128)} copy(f32[128,2048]{1,0:T(8,128)} %get-tuple-element.16) | data formatting | bytes 2097152 | tf_op jit(solution)/shard_map/jit(_where)/select_n | solution.py:256
  119.4 1.3 divide_convert_fusion
  121.4 0.5 copy-done.8
  121.9 0.6 copy-done.2
  122.5 1.2 fusion.10
  123.7 2.1 copy.34
  125.8 1.3 copy.29
  127.1 2.5 %fusion.51 = f32[16,128,128]{2,1,0:T(8,128)} fusion(bf16[128,16,128]{0,2,1:T(8,128)(2,1)S(1)} %copy.24, bf16[16,128,128]{1,2,0:T(8,128)(2,1)} %copy-done.8), kind=kOutput, calls=%fused_computation.77 | convolution fusion | flops 67108864 | bytes 2097152 | tf_op jit(solution)/shard_map/hts,thd->shd/dot_general | solution.py:310
  129.6 0.5 fusion.23
  130.2 0.5 fusion.52
  130.6 1.1 select_maximum_fusion.s_ref
  131.7 107.1 %scan_rev.1 = f32[2,1088,128]{2,1,0:T(8,128)} custom-call(f32[2,1088,128]{2,1,0:T(8,128)} %select_maximum_fusion.s_ref), custom_call_target="tpu_custom_call" | custom-call | tf_op jit(solution)/shard_map/scan_rev/pallas_call | solution.py:237
  238.8 1.4 slice.24
  240.2 0.7 slice_bitcast_fusion
  240.9 0.5 fusion.11
  241.5 1.0 copy.35
  242.5 0.5 fusion.41
  243.0 0.6 copy-done.7
  243.5 0.5 fusion.12
  244.0 1.0 copy.36
  (31 shorter events, 2.2 us)
Async XLA Ops:
  0.6 7.4 %copy-start = (bf16[128,2048]{1,0:T(8,128)(2,1)S(1)}, bf16[128,2048]{1,0:T(8,128)(2,1)}, u32[]{:S(2)}) copy-start(bf16[128,2048]{1,0:T(8,128)(2,1)} %param.6) | copy-start | bytes 1572868
  0.6 2.3 copy-start.9
  6.1 1.3 copy-start.6
  114.1 1.2 copy-start.5
  114.1 1.3 copy-start.10
  121.1 0.8 copy-start.8
  121.1 1.4 copy-start.2
  123.7 2.1 copy-start.1
  131.7 109.2 %copy-start.3 = (f32[128,2048]{0,1:T(8,128)S(1)}, f32[128,2048]{0,1:T(8,128)}, u32[]{:S(2)}) copy-start(f32[128,2048]{0,1:T(8,128)} %copy.29) | copy-start | bytes 3145732
  238.8 2.1 copy-start.4
  241.4 1.0 copy-start.11
  242.5 1.0 copy-start.7

commit v2 on v0

v2 whole, which is shorter than its diff:
```python
import functools

import jax
import jax.numpy as jnp
from jax import lax
from jax.experimental import pallas as pl
from jax.experimental.pallas import tpu as pltpu
from jax.sharding import PartitionSpec as P

HEADS = 16
HD = 128
TOK = 128
NZ, NX, NY = 16, 4, 4
MESH = pl.DeviceIdType.MESH
CHUNK = 64
PER_HEAD = HD // CHUNK
N = 1 + HEADS * PER_HEAD
SUBSTEP = 4
F32 = jnp.float32
BF16 = jnp.bfloat16


def features(x):
    wide = x.astype(F32)
    return jnp.where(wide > 0, wide + 1.0, jnp.exp(jnp.minimum(wide, 0.0)))


def slope(x):
    wide = x.astype(F32)
    return jnp.where(wide > 0, 1.0, jnp.exp(jnp.minimum(wide, 0.0)))


def mul(a, b, da, db):
    return lax.dot_general(a, b, (((da,), (db,)), ((), ())), preferred_element_type=F32)


class Scan:
    def __init__(self, rev, s, p, bufs, rs, ss):
        self.s, self.p, self.rs, self.ss = s, p, rs, ss
        (self.oth, self.zin, self.zout, self.tin, self.yin, self.yout, self.xpin, self.xpout,
         self.xmin, self.xmout, self.cin, self.cout) = bufs
        z = lax.axis_index("inner")
        outer = lax.axis_index("outer")
        core = lax.rem(outer, 2)
        x = lax.rem(outer // 2, NX)
        y = outer // (2 * NX)
        flip = (lambda v, m: m - 1 - v) if rev else (lambda v, m: v)
        self.xc, self.yc, self.cc = flip(x, NX), flip(y, NY), flip(core, 2)
        zc = flip(z, NZ)
        step = -1 if rev else 1

        def dev(y_, x_, c_, z_):
            return {"outer": (y_ * NX + x_) * 2 + c_, "inner": z_}

        zstep = jnp.where(self.cc == 0, step, -step)
        self.zpos = jnp.where(self.cc == 0, zc, NZ - 1 - zc)
        self.d_zn = dev(y, x, core, lax.rem(z + zstep + NZ, NZ))
        self.d_zp = dev(y, x, core, lax.rem(z - zstep + NZ, NZ))
        self.d_xn = dev(y, lax.rem(x + step + NX, NX), core, z)
        self.d_xp = dev(y, lax.rem(x - step + NX, NX), core, z)
        self.d_yn = dev(lax.rem(y + step + NY, NY), x, core, z)
        self.d_yp = dev(lax.rem(y - step + NY, NY), x, core, z)
        self.d_oc = dev(y, x, 1 - core, z)

    def clear(self):
        def zero(where, ref):
            @pl.when(where)
            def _():
                ref[...] = jnp.zeros_like(ref)

        zero(self.zpos == 0, self.zin)
        zero(self.yc == 0, self.yin)
        zero(self.xc == 0, self.xpin)
        zero(self.xc == NX - 1, self.xmin)

    def rc(self, k, src, dst, d, i):
        return pltpu.make_async_remote_copy(src_ref=src, dst_ref=dst, send_sem=self.ss.at[k], recv_sem=self.rs.at[k, i], device_id=d, device_id_type=MESH)

    def ex(self, i):
        return self.rc(0, self.s.at[i], self.oth.at[i], self.d_oc, i)

    def zz(self, i):
        return self.rc(1, self.zout.at[i], self.zin.at[i], self.d_zn, i)

    def tu(self, i):
        return self.rc(2, self.zin.at[i, 1], self.tin.at[i], self.d_oc, i)

    def td(self, i):
        return self.rc(2, self.zout.at[i, 1], self.tin.at[i], self.d_oc, i)

    def yy(self, i):
        return self.rc(3, self.yout.at[i], self.yin.at[i], self.d_yn, i)

    def xpl(self, i):
        return self.rc(4, self.xpout.at[i], self.xpin.at[i], self.d_xn, i)

    def xmi(self, i):
        return self.rc(5, self.xmout.at[i], self.xmin.at[i], self.d_xp, i)

    def ce(self, i):
        return self.rc(6, self.cout.at[i], self.cin.at[i], self.d_oc, i)

    def step_z(self, i):
        cc, zin, zout = self.cc, self.zin, self.zout
        self.ex(i).wait_recv()

        @pl.when(self.zpos > 0)
        def _():
            self.zz(i).wait_recv()

        @pl.when(cc == 0)
        def _():
            self.tu(i).start()

        own = self.s[i]
        other = self.oth[i]
        zout[i, 0] = zin[i, 0] + jnp.where(cc == 0, own, other)
        zout[i, 1] = zin[i, 1] + (own + other)

        @pl.when(self.zpos < NZ - 1)
        def _():
            self.zz(i).start()

        @pl.when(jnp.logical_and(cc == 1, lax.rem(i, 2) == 0))
        def _():
            self.td(i).start()

    def step_y(self, i):
        self.tu(i).wait_recv()

        @pl.when(self.yc > 0)
        def _():
            self.yy(i).wait_recv()

        self.yout[i] = self.yin[i] + (self.tin[i] + jnp.where(self.cc == 0, self.zin[i, 1], self.zout[i, 1]))

        @pl.when(self.yc < NY - 1)
        def _():
            self.yy(i).start()

    def step_xp(self, i):
        @pl.when(self.xc > 0)
        def _():
            self.xpl(i).wait_recv()

        self.xpout[i] = self.xpin[i] + self.yout[i]

        @pl.when(self.xc < NX - 1)
        def _():
            self.xpl(i).start()

    def step_xm(self, i):
        @pl.when(self.xc < NX - 1)
        def _():
            self.xmi(i).wait_recv()

        self.xmout[i] = self.xmin[i] + self.yin[i]

        @pl.when(self.xc > 0)
        def _():
            self.xmi(i).start()

    def column(self, i):
        return jnp.where(self.cc == 0, self.zin[i, 0], self.tin[i] + self.zout[i, 0])

    def step_f(self, i):
        c = self.xpin[i] + self.xmout[i]
        self.cout[i] = c
        self.ce(i).start()
        self.p[i] = c + self.column(i)

    def run(self):
        cc = self.cc
        l_y = jnp.where(self.zpos < NZ // 2, N, 1 + SUBSTEP * self.yc)
        l_xp = l_y + SUBSTEP * self.xc
        l_xm = l_y + SUBSTEP * (NX - 1 - self.xc)
        l_f = jnp.maximum(l_xp, l_xm)

        def slot(t, carry):
            @pl.when(t < N)
            def _():
                self.step_z(t)

            def later(lag, f):
                i = t - lag

                @pl.when((i >= 0) & (i < N) & (lax.rem(i + 2 * N, 2) == cc))
                def _():
                    f(i)

            later(l_y, self.step_y)
            later(l_xp, self.step_xp)
            later(l_xm, self.step_xm)
            later(l_f, self.step_f)
            return carry

        lax.fori_loop(0, N + l_f, slot, 0)

    def finish(self, i):
        @pl.when(lax.rem(i, 2) != self.cc)
        def _():
            @pl.when(self.cc == 1)
            def _():
                self.tu(i).wait_recv()

            self.ce(i).wait_recv()
            self.p[i] = self.cin[i] + self.column(i)

    def drain(self):
        def whole(k, buf, d):
            pltpu.make_async_remote_copy(src_ref=buf, dst_ref=buf, send_sem=self.ss.at[k], recv_sem=self.rs.at[k, 0], device_id=d, device_id_type=MESH).wait_send()

        def mine(k, buf, d, where):
            @pl.when(where & (self.cc == 0))
            def _():
                whole(k, buf.at[pl.ds(0, N - N // 2)], d)

            @pl.when(where & (self.cc == 1))
            def _():
                whole(k, buf.at[pl.ds(0, N // 2)], d)

        whole(0, self.oth, self.d_oc)

        @pl.when(self.zpos < NZ - 1)
        def _():
            whole(1, self.zout, self.d_zn)

        @pl.when(self.cc == 0)
        def _():
            whole(2, self.tin, self.d_oc)

        @pl.when(self.cc == 1)
        def _():
            whole(2, self.tin.at[pl.ds(0, N - N // 2)], self.d_oc)

        mine(3, self.yout, self.d_yn, self.yc < NY - 1)
        mine(4, self.xpout, self.d_xn, self.xc < NX - 1)
        mine(5, self.xmout, self.d_xp, self.xc > 0)
        mine(6, self.cout, self.d_oc, self.cc >= 0)


N_BUFS = 12


def kernel(q_ref, k_ref, v_ref, g_ref, att_ref, qg_ref, kg_ref, vg_ref, qf_ref, kf_ref, ki_ref, vi_ref, s1, p1, s2, p2, *rest):
    bufs1, bufs2 = rest[:N_BUFS], rest[N_BUFS : 2 * N_BUFS]
    rs1, ss1, rs2, ss2 = rest[2 * N_BUFS :]
    one = Scan(False, s1, p1, bufs1, rs1, ss1)
    two = Scan(True, s2, p2, bufs2, rs2, ss2)
    near = (one.d_zn, one.d_zp, one.d_xn, one.d_xp, one.d_yn, one.d_yp, one.d_oc)
    bar = pltpu.get_barrier_semaphore()
    for d in near:
        pl.semaphore_signal(bar, inc=1, device_id=d, device_id_type=MESH)
    s1[0] = jnp.zeros((CHUNK, HD), F32)
    s2[0] = jnp.zeros((CHUNK, HD), F32)

    def cols(h):
        return pl.ds(pl.multiple_of(h * HD, HD), HD)

    def put(s, h, state):
        for j in range(PER_HEAD):
            s[1 + h * PER_HEAD + j] = state[j * CHUNK : (j + 1) * CHUNK]

    def get(p, h):
        return jnp.concatenate([p[1 + h * PER_HEAD + j] for j in range(PER_HEAD)], axis=0)

    @pl.loop(0, HEADS)
    def _(h):
        kf = features(k_ref[:, cols(h)]).astype(BF16)
        kf_ref[:, cols(h)] = kf
        qf_ref[:, cols(h)] = features(q_ref[:, cols(h)]).astype(BF16)
        s1[0, pl.ds(h, 1), :] = jnp.sum(kf.astype(F32), axis=0, keepdims=True)
        put(s1, h, mul(kf, v_ref[:, cols(h)], 0, 0))

    one.clear()
    two.clear()
    pl.semaphore_wait(bar, len(near))

    @pl.loop(0, N)
    def _(i):
        one.ex(i).start()

    one.run()
    one.finish(0)
    rows = lax.broadcasted_iota(jnp.int32, (TOK, TOK), 0)
    lanes = lax.broadcasted_iota(jnp.int32, (TOK, TOK), 1)
    causal = lanes <= rows

    @pl.loop(0, HEADS)
    def _(h):
        for j in range(PER_HEAD):
            one.finish(1 + h * PER_HEAD + j)
        c = cols(h)
        qf, kf, v = qf_ref[:, c], kf_ref[:, c], v_ref[:, c]
        wide_q = qf.astype(F32)
        normal = p1[0, pl.ds(h, 1), :]
        low = get(p1, h).astype(BF16)
        scores = jnp.where(causal, mul(qf, kf, 1, 1), 0.0)
        weights = scores.astype(BF16)
        den = jnp.sum(scores, axis=1, keepdims=True) + jnp.sum(wide_q * normal, axis=1, keepdims=True)
        num = mul(weights, v, 1, 0) + mul(qf, low, 1, 0)
        ratio = num / den
        att_ref[:, c] = ratio.astype(BF16)
        cot = g_ref[:, c].astype(F32)
        scaled = (cot / den).astype(BF16)
        grad_den = -jnp.sum(cot * ratio, axis=1, keepdims=True) / den
        grad_scores = jnp.where(causal, mul(scaled, v, 1, 1) + grad_den, 0.0).astype(BF16)
        put(s2, h, mul(qf, scaled, 0, 0))
        s2[0, pl.ds(h, 1), :] = jnp.sum(grad_den * wide_q, axis=0, keepdims=True)
        for j in range(PER_HEAD):
            two.ex(1 + h * PER_HEAD + j).start()
        lin = mul(grad_scores, kf, 1, 0) + mul(scaled, low, 1, 1) + grad_den * normal
        qg_ref[:, c] = (lin * slope(q_ref[:, c])).astype(BF16)
        ki_ref[:, c] = mul(grad_scores, qf, 0, 0)
        vi_ref[:, c] = mul(weights, scaled, 0, 0)

    two.ex(0).start()
    two.run()
    two.finish(0)

    @pl.loop(0, HEADS)
    def _(h):
        for j in range(PER_HEAD):
            two.finish(1 + h * PER_HEAD + j)
        c = cols(h)
        low = get(p2, h).astype(BF16)
        lin = ki_ref[:, c] + mul(v_ref[:, c], low, 1, 1) + p2[0, pl.ds(h, 1), :]
        kg_ref[:, c] = (lin * slope(k_ref[:, c])).astype(BF16)
        vg_ref[:, c] = (vi_ref[:, c] + mul(kf_ref[:, c], low, 1, 0)).astype(BF16)

    one.drain()
    two.drain()


def per_device(queries, keys, values, cotangent):
    wide = HEADS * HD
    single = pltpu.VMEM((N, CHUNK, HD), F32)
    double = pltpu.VMEM((N, 2, CHUNK, HD), F32)
    bufs = [single, double, double] + [single] * (N_BUFS - 3)
    low = pltpu.VMEM((TOK, wide), BF16)
    full = pltpu.VMEM((TOK, wide), F32)
    sems = [pltpu.SemaphoreType.DMA((7, N)), pltpu.SemaphoreType.DMA((7,))]
    vmem = pl.BlockSpec(memory_space=pltpu.VMEM)
    return pl.pallas_call(
        kernel,
        out_shape=[jax.ShapeDtypeStruct((TOK, wide), BF16)] * 4,
        in_specs=[vmem] * 4,
        out_specs=[vmem] * 4,
        scratch_shapes=[low, low, full, full] + [single] * 4 + bufs * 2 + sems * 2,
        compiler_params=pltpu.CompilerParams(collective_id=0, has_side_effects=True, vmem_limit_bytes=63 << 20),
        name="linear_attention",
    )(queries, keys, values, cotangent)


def solution(mesh):
    spec = P(("outer", "inner"), None)
    return jax.shard_map(per_device, mesh=mesh, in_specs=(spec,) * 4, out_specs=(spec,) * 4, check_vma=False)
```

time: 851 us -> 212 us (0.25); the launches traced: 836 us -> 211 us
  waiting for transfers between devices: 441 us -> 0 us
  blocking collectives: 218 us -> 0 us
  Pallas kernels: 0 us -> 205 us
  other arithmetic: 116 us -> 0 us
  matrix products: 22.3 us -> 0 us
  local copies, waits for them, and re-layouts: 20.7 us -> 5.19 us
  between operations: 14.5 us -> 0.65 us
    all_gather x6 -> x0, waiting for transfers between devices: 314 us -> none  [the longest x4 215 us: entering(): everything = jax.tree.map(lambda part: lax.all_gather(part, axis), shard)]
    pallas_call x0 -> x1, Pallas kernels: none -> 205 us  [per_device(): pl.pallas_call(kernel, out_shape=[jax.ShapeDtypeStruct((TOK, wide), BF16)...]
    all_gather x6 -> x0, blocking collectives: 173 us -> none  [the longest x4 123 us: entering(): everything = jax.tree.map(lambda part: lax.all_gather(part, axis), shard)]
    reduce_scatter x2 -> x0, waiting for transfers between devices: 125 us -> none  [carry_states(): lax.psum_scatter(parts[0], 'inner', scatter_dimension=0, tiled=True)]
    select_n x194 -> x0, other arithmetic: 112 us -> none  [the longest x192 107 us: lap(): return jax.tree.map(lambda a, b: jnp.where(reached, a, b), new, before)]
    unnamed x2 -> x0, blocking collectives: 45.2 us -> none
    dot_general x14 -> x0, matrix products: 22.3 us -> none  [the longest x1 2.6 us: per_device(): jnp.einsum('hts,she->the', weights, value_rows, preferred_element_type=f32)]
  transfers between devices with their start and end apart: 8 -> 0, of which waited for: 6 -> 0; matrix products, arithmetic and copies ran while one was open for 14% -> 0% of each run, Pallas kernels for 0% -> 0%
where the time goes in v2:
time: 212 us; the launch traced here: 211 us
  Pallas kernels  205 us (97%)
  local copies, waits for them, and re-layouts  5.19 us (2%)
    pallas_call x1, Pallas kernels, per_device(): pl.pallas_call(kernel, out_shape=[jax.ShapeDtypeStruct((TOK, wide), BF16)...  205 us
    unnamed x10, local copies, waits for them, and re-layouts  5.19 us

profile of v2, /device:TPU:1, one launch (start us, length us, event | category | flops | bytes accessed | tf_op | source)
XLA Modules:
  0.0 210.8 jit_solution(12981316641184866983)
XLA Ops:
  0.6 204.9 %linear_attention.1 = (bf16[128,2048]{1,0:T(8,128)(2,1)}, bf16[128,2048]{1,0:T(8,128)(2,1)}, bf16[128,2048]{1,0:T(8,128)(2,1)}, bf16[128,2048]{1,0:T(8,128)(2,1)}) custom-call(bf16[128,2048]{1,0:T(8,128)(2,1)} %q_ref.1, bf16[128,2048]{1,0:T(8,128)(2,1)} %k_ref.1, bf16[128,2048]{1,0:T(8,128)(2,1)} %v_ref.1, bf16[128,2048]{1,0:T(8,128)(2,1)} %g_ref.1), custom_call_target="tpu_custom_call" | custom-call | tf_op jit(solution)/shard_map/linear_attention/pallas_call | solution.py:344
  205.6 0.0 copy-start.2
  205.6 1.9 copy.12
  207.5 0.0 copy-done.2
  207.5 0.0 copy-start.1
  207.5 0.8 copy.13
  208.3 0.4 copy-done.1
  208.8 0.0 copy-start
  208.8 0.8 copy.14
  209.6 0.4 copy-done
  210.0 0.8 copy.15
Async XLA Ops:
  205.6 2.0 copy-start.2
  207.5 1.2 copy-start.1
  208.8 1.2 copy-start

commit v3 on v2

--- a/solution.py
+++ b/solution.py
@@ -15,7 +15,8 @@
 CHUNK = 64
 PER_HEAD = HD // CHUNK
 N = 1 + HEADS * PER_HEAD
-SUBSTEP = 4
+SUBSTEP = 3
+EARLY = 50
 F32 = jnp.float32
 BF16 = jnp.bfloat16
 
@@ -169,32 +170,30 @@
         self.ce(i).start()
         self.p[i] = c + self.column(i)
 
-    def run(self):
-        cc = self.cc
-        l_y = jnp.where(self.zpos < NZ // 2, N, 1 + SUBSTEP * self.yc)
+    def lags(self):
+        late = self.zpos >= NZ // 2
+        l_y = jnp.where(late, 1, jnp.minimum(N, EARLY * (NZ - 1 - 2 * self.zpos))) + SUBSTEP * self.yc
         l_xp = l_y + SUBSTEP * self.xc
         l_xm = l_y + SUBSTEP * (NX - 1 - self.xc)
-        l_f = jnp.maximum(l_xp, l_xm)
-
-        def slot(t, carry):
-            @pl.when(t < N)
-            def _():
-                self.step_z(t)
-
-            def later(lag, f):
-                i = t - lag
-
-                @pl.when((i >= 0) & (i < N) & (lax.rem(i + 2 * N, 2) == cc))
-                def _():
-                    f(i)
-
-            later(l_y, self.step_y)
-            later(l_xp, self.step_xp)
-            later(l_xm, self.step_xm)
-            later(l_f, self.step_f)
-            return carry
-
-        lax.fori_loop(0, N + l_f, slot, 0)
+        return l_y, l_xp, l_xm, jnp.maximum(l_xp, l_xm)
+
+    def slot(self, t):
+        @pl.when((t >= 0) & (t < N))
+        def _():
+            self.step_z(t)
+
+        def later(lag, f):
+            i = t - lag
+
+            @pl.when((i >= 0) & (i < N) & (lax.rem(i + 8 * N, 2) == self.cc))
+            def _():
+                f(i)
+
+        l_y, l_xp, l_xm, l_f = self.lags()
+        later(l_y, self.step_y)
+        later(l_xp, self.step_xp)
+        later(l_xm, self.step_xm)
+        later(l_f, self.step_f)
 
     def finish(self, i):
         @pl.when(lax.rem(i, 2) != self.cc)
@@ -252,17 +251,17 @@
     for d in near:
         pl.semaphore_signal(bar, inc=1, device_id=d, device_id_type=MESH)
     s1[0] = jnp.zeros((CHUNK, HD), F32)
-    s2[0] = jnp.zeros((CHUNK, HD), F32)
+    s2[N - 1] = jnp.zeros((CHUNK, HD), F32)
 
     def cols(h):
         return pl.ds(pl.multiple_of(h * HD, HD), HD)
 
-    def put(s, h, state):
+    def put(s, i, state):
         for j in range(PER_HEAD):
-            s[1 + h * PER_HEAD + j] = state[j * CHUNK : (j + 1) * CHUNK]
-
-    def get(p, h):
-        return jnp.concatenate([p[1 + h * PER_HEAD + j] for j in range(PER_HEAD)], axis=0)
+            s[i + j] = state[j * CHUNK : (j + 1) * CHUNK]
+
+    def get(p, i):
+        return jnp.concatenate([p[i + j] for j in range(PER_HEAD)], axis=0)
 
     @pl.loop(0, HEADS)
     def _(h):
@@ -270,7 +269,7 @@
         kf_ref[:, cols(h)] = kf
         qf_ref[:, cols(h)] = features(q_ref[:, cols(h)]).astype(BF16)
         s1[0, pl.ds(h, 1), :] = jnp.sum(kf.astype(F32), axis=0, keepdims=True)
-        put(s1, h, mul(kf, v_ref[:, cols(h)], 0, 0))
+        put(s1, 1 + h * PER_HEAD, mul(kf, v_ref[:, cols(h)], 0, 0))
 
     one.clear()
     two.clear()
@@ -280,21 +279,16 @@
     def _(i):
         one.ex(i).start()
 
-    one.run()
-    one.finish(0)
     rows = lax.broadcasted_iota(jnp.int32, (TOK, TOK), 0)
     lanes = lax.broadcasted_iota(jnp.int32, (TOK, TOK), 1)
     causal = lanes <= rows
 
-    @pl.loop(0, HEADS)
-    def _(h):
-        for j in range(PER_HEAD):
-            one.finish(1 + h * PER_HEAD + j)
+    def middle(h):
         c = cols(h)
         qf, kf, v = qf_ref[:, c], kf_ref[:, c], v_ref[:, c]
         wide_q = qf.astype(F32)
         normal = p1[0, pl.ds(h, 1), :]
-        low = get(p1, h).astype(BF16)
+        low = get(p1, 1 + h * PER_HEAD).astype(BF16)
         scores = jnp.where(causal, mul(qf, kf, 1, 1), 0.0)
         weights = scores.astype(BF16)
         den = jnp.sum(scores, axis=1, keepdims=True) + jnp.sum(wide_q * normal, axis=1, keepdims=True)
@@ -304,29 +298,66 @@
         cot = g_ref[:, c].astype(F32)
         scaled = (cot / den).astype(BF16)
         grad_den = -jnp.sum(cot * ratio, axis=1, keepdims=True) / den
+        put(s2, h * PER_HEAD, mul(qf, scaled, 0, 0))
+        s2[N - 1, pl.ds(h, 1), :] = jnp.sum(grad_den * wide_q, axis=0, keepdims=True)
+        for j in range(PER_HEAD):
+            two.ex(h * PER_HEAD + j).start()
+
+        @pl.when(h == HEADS - 1)
+        def _():
+            two.ex(N - 1).start()
+
         grad_scores = jnp.where(causal, mul(scaled, v, 1, 1) + grad_den, 0.0).astype(BF16)
-        put(s2, h, mul(qf, scaled, 0, 0))
-        s2[0, pl.ds(h, 1), :] = jnp.sum(grad_den * wide_q, axis=0, keepdims=True)
-        for j in range(PER_HEAD):
-            two.ex(1 + h * PER_HEAD + j).start()
         lin = mul(grad_scores, kf, 1, 0) + mul(scaled, low, 1, 1) + grad_den * normal
         qg_ref[:, c] = (lin * slope(q_ref[:, c])).astype(BF16)
         ki_ref[:, c] = mul(grad_scores, qf, 0, 0)
         vi_ref[:, c] = mul(weights, scaled, 0, 0)
 
-    two.ex(0).start()
-    two.run()
-    two.finish(0)
+    def last(h):
+        c = cols(h)
+        low = get(p2, h * PER_HEAD).astype(BF16)
+        ki_ref[:, c] += mul(v_ref[:, c], low, 1, 1)
+        vg_ref[:, c] = (vi_ref[:, c] + mul(kf_ref[:, c], low, 1, 0)).astype(BF16)
+
+    zpos = one.zpos
+    late = zpos >= NZ // 2
+    behind = 2 * zpos - (NZ - 1)
+    l_f1, l_f2 = one.lags()[3], two.lags()[3]
+    l_g1 = l_f1 + 1 + jnp.where(late, jnp.maximum(0, N - 4 * behind // 2), 0)
+    l_b = l_g1 + 6 + jnp.where(late, jnp.minimum(N, 18 + 5 * (zpos - NZ // 2)), jnp.minimum(6 * zpos, 14))
+    l_g2 = l_b + l_f2 + 2 + jnp.where(late, jnp.maximum(0, N - 6 * behind // 2), 0)
+
+    def slot(t, carry):
+        one.slot(t)
+        i = t - l_g1
+
+        @pl.when((i >= 0) & (i < N))
+        def _():
+            one.finish(i)
+
+            @pl.when((i > 0) & (lax.rem(i, PER_HEAD) == 0))
+            def _():
+                middle(i // PER_HEAD - 1)
+
+        two.slot(t - l_b)
+        k = t - l_g2
+
+        @pl.when((k >= 0) & (k < N))
+        def _():
+            two.finish(k)
+
+            @pl.when((k < N - 1) & (lax.rem(k + 1, PER_HEAD) == 0))
+            def _():
+                last(k // PER_HEAD)
+
+        return carry
+
+    lax.fori_loop(0, N + l_g2, slot, 0)
 
     @pl.loop(0, HEADS)
     def _(h):
-        for j in range(PER_HEAD):
-            two.finish(1 + h * PER_HEAD + j)
         c = cols(h)
-        low = get(p2, h).astype(BF16)
-        lin = ki_ref[:, c] + mul(v_ref[:, c], low, 1, 1) + p2[0, pl.ds(h, 1), :]
-        kg_ref[:, c] = (lin * slope(k_ref[:, c])).astype(BF16)
-        vg_ref[:, c] = (vi_ref[:, c] + mul(kf_ref[:, c], low, 1, 0)).astype(BF16)
+        kg_ref[:, c] = ((ki_ref[:, c] + p2[N - 1, pl.ds(h, 1), :]) * slope(k_ref[:, c])).astype(BF16)
 
     one.drain()
     two.drain()

time: 212 us -> 191 us (0.901)
  Pallas kernels: 205 us -> 185 us
    pallas_call x1, Pallas kernels: 205 us -> 185 us  [per_device(): pl.pallas_call(kernel, out_shape=[jax.ShapeDtypeStruct((TOK, wide), BF16)...]
where the time goes in v3:
time: 191 us
  Pallas kernels  185 us (97%)
  local copies, waits for them, and re-layouts  5.19 us (3%)
    pallas_call x1, Pallas kernels, per_device(): pl.pallas_call(kernel, out_shape=[jax.ShapeDtypeStruct((TOK, wide), BF16)...  185 us
    unnamed x10, local copies, waits for them, and re-layouts  5.19 us

profile of v3, /device:TPU:1, one launch (start us, length us, event | category | flops | bytes accessed | tf_op | source)
XLA Modules:
  0.0 191.0 jit_solution(7127802396356363683)
XLA Ops:
  0.6 185.2 %linear_attention.1 = (bf16[128,2048]{1,0:T(8,128)(2,1)}, bf16[128,2048]{1,0:T(8,128)(2,1)}, bf16[128,2048]{1,0:T(8,128)(2,1)}, bf16[128,2048]{1,0:T(8,128)(2,1)}) custom-call(bf16[128,2048]{1,0:T(8,128)(2,1)} %q_ref.1, bf16[128,2048]{1,0:T(8,128)(2,1)} %k_ref.1, bf16[128,2048]{1,0:T(8,128)(2,1)} %v_ref.1, bf16[128,2048]{1,0:T(8,128)(2,1)} %g_ref.1), custom_call_target="tpu_custom_call" | custom-call | tf_op jit(solution)/shard_map/linear_attention/pallas_call | solution.py:375
  185.8 0.0 copy-start.2
  185.8 1.9 %copy.12 = bf16[128,2048]{1,0:T(8,128)(2,1)} copy(bf16[128,2048]{1,0:T(8,128)(2,1)} %get-tuple-element.8) | data formatting | bytes 1048576
  187.8 0.0 copy-done.2
  187.8 0.0 copy-start.1
  187.8 0.8 copy.13
  188.6 0.4 copy-done.1
  189.0 0.0 copy-start
  189.0 0.8 copy.14
  189.8 0.4 copy-done
  190.2 0.8 copy.15
Async XLA Ops:
  185.8 2.0 %copy-start.2 = (bf16[128,2048]{1,0:T(8,128)(2,1)S(1)}, bf16[128,2048]{1,0:T(8,128)(2,1)}, u32[]{:S(2)}) copy-start(bf16[128,2048]{1,0:T(8,128)(2,1)} %get-tuple-element.9) | copy-start | bytes 1572868
  187.8 1.2 copy-start.1
  189.0 1.2 copy-start

commit v4 on v3

--- a/solution.py
+++ b/solution.py
@@ -241,7 +241,7 @@
 N_BUFS = 12
 
 
-def kernel(q_ref, k_ref, v_ref, g_ref, att_ref, qg_ref, kg_ref, vg_ref, qf_ref, kf_ref, ki_ref, vi_ref, s1, p1, s2, p2, *rest):
+def kernel(q_ref, k_ref, v_ref, g_ref, att_ref, qg_ref, kg_ref, vg_ref, qf_ref, kf_ref, ki_ref, vi_ref, w_ref, gs_ref, den_ref, gd_ref, s1, p1, s2, p2, *rest):
     bufs1, bufs2 = rest[:N_BUFS], rest[N_BUFS : 2 * N_BUFS]
     rs1, ss1, rs2, ss2 = rest[2 * N_BUFS :]
     one = Scan(False, s1, p1, bufs1, rs1, ss1)
@@ -283,21 +283,29 @@
     lanes = lax.broadcasted_iota(jnp.int32, (TOK, TOK), 1)
     causal = lanes <= rows
 
+    def before(h):
+        c = cols(h)
+        scores = jnp.where(causal, mul(qf_ref[:, c], kf_ref[:, c], 1, 1), 0.0)
+        weights = scores.astype(BF16)
+        w_ref[:, c] = weights
+        den_ref[h] = jnp.sum(scores, axis=1, keepdims=True)
+        vi_ref[:, c] = mul(weights, v_ref[:, c], 1, 0)
+
     def middle(h):
         c = cols(h)
-        qf, kf, v = qf_ref[:, c], kf_ref[:, c], v_ref[:, c]
+        qf = qf_ref[:, c]
         wide_q = qf.astype(F32)
         normal = p1[0, pl.ds(h, 1), :]
         low = get(p1, 1 + h * PER_HEAD).astype(BF16)
-        scores = jnp.where(causal, mul(qf, kf, 1, 1), 0.0)
-        weights = scores.astype(BF16)
-        den = jnp.sum(scores, axis=1, keepdims=True) + jnp.sum(wide_q * normal, axis=1, keepdims=True)
-        num = mul(weights, v, 1, 0) + mul(qf, low, 1, 0)
+        den = den_ref[h] + jnp.sum(wide_q * normal, axis=1, keepdims=True)
+        num = vi_ref[:, c] + mul(qf, low, 1, 0)
         ratio = num / den
         att_ref[:, c] = ratio.astype(BF16)
         cot = g_ref[:, c].astype(F32)
         scaled = (cot / den).astype(BF16)
         grad_den = -jnp.sum(cot * ratio, axis=1, keepdims=True) / den
+        gs_ref[:, c] = scaled
+        gd_ref[h] = grad_den
         put(s2, h * PER_HEAD, mul(qf, scaled, 0, 0))
         s2[N - 1, pl.ds(h, 1), :] = jnp.sum(grad_den * wide_q, axis=0, keepdims=True)
         for j in range(PER_HEAD):
@@ -307,11 +315,16 @@
         def _():
             two.ex(N - 1).start()
 
+    def after(h):
+        c = cols(h)
+        qf, kf, v, scaled, grad_den = qf_ref[:, c], kf_ref[:, c], v_ref[:, c], gs_ref[:, c], gd_ref[h]
+        normal = p1[0, pl.ds(h, 1), :]
+        low = get(p1, 1 + h * PER_HEAD).astype(BF16)
         grad_scores = jnp.where(causal, mul(scaled, v, 1, 1) + grad_den, 0.0).astype(BF16)
         lin = mul(grad_scores, kf, 1, 0) + mul(scaled, low, 1, 1) + grad_den * normal
         qg_ref[:, c] = (lin * slope(q_ref[:, c])).astype(BF16)
         ki_ref[:, c] = mul(grad_scores, qf, 0, 0)
-        vi_ref[:, c] = mul(weights, scaled, 0, 0)
+        vi_ref[:, c] = mul(w_ref[:, c], scaled, 0, 0)
 
     def last(h):
         c = cols(h)
@@ -324,13 +337,21 @@
     behind = 2 * zpos - (NZ - 1)
     l_f1, l_f2 = one.lags()[3], two.lags()[3]
     l_g1 = l_f1 + 1 + jnp.where(late, jnp.maximum(0, N - 4 * behind // 2), 0)
-    l_b = l_g1 + 6 + jnp.where(late, jnp.minimum(N, 18 + 5 * (zpos - NZ // 2)), jnp.minimum(6 * zpos, 14))
+    l_b = l_g1 + 6 + jnp.where(late, jnp.minimum(N, 33 + 5 * (zpos - NZ // 2)), jnp.minimum(6 * zpos, 33))
     l_g2 = l_b + l_f2 + 2 + jnp.where(late, jnp.maximum(0, N - 6 * behind // 2), 0)
 
+    t_before = jnp.where(zpos >= 4, 0, N)
+    t_after = jnp.where(late, l_b, l_b + N)
+
     def slot(t, carry):
+        @pl.when(t == t_before)
+        def _():
+            pl.loop(0, HEADS)(before)
+
         one.slot(t)
         i = t - l_g1
 
+
         @pl.when((i >= 0) & (i < N))
         def _():
             one.finish(i)
@@ -338,6 +359,7 @@
             @pl.when((i > 0) & (lax.rem(i, PER_HEAD) == 0))
             def _():
                 middle(i // PER_HEAD - 1)
+                after(i // PER_HEAD - 1)
 
         two.slot(t - l_b)
         k = t - l_g2
@@ -370,6 +392,7 @@
     bufs = [single, double, double] + [single] * (N_BUFS - 3)
     low = pltpu.VMEM((TOK, wide), BF16)
     full = pltpu.VMEM((TOK, wide), F32)
+    thin = pltpu.VMEM((HEADS, TOK, 1), F32)
     sems = [pltpu.SemaphoreType.DMA((7, N)), pltpu.SemaphoreType.DMA((7,))]
     vmem = pl.BlockSpec(memory_space=pltpu.VMEM)
     return pl.pallas_call(
@@ -377,7 +400,7 @@
         out_shape=[jax.ShapeDtypeStruct((TOK, wide), BF16)] * 4,
         in_specs=[vmem] * 4,
         out_specs=[vmem] * 4,
-        scratch_shapes=[low, low, full, full] + [single] * 4 + bufs * 2 + sems * 2,
+        scratch_shapes=[low, low, full, full, low, low, thin, thin] + [single] * 4 + bufs * 2 + sems * 2,
         compiler_params=pltpu.CompilerParams(collective_id=0, has_side_effects=True, vmem_limit_bytes=63 << 20),
         name="linear_attention",
     )(queries, keys, values, cotangent)

time: 191 us -> 192 us (level)
  no operation moved by 1% of the time
where the time goes in v4:
time: 192 us; the launch traced here: 191 us
  Pallas kernels  186 us (97%)
  local copies, waits for them, and re-layouts  5.19 us (3%)
    pallas_call x1, Pallas kernels, per_device(): pl.pallas_call(kernel, out_shape=[jax.ShapeDtypeStruct((TOK, wide), BF16)...  186 us
    unnamed x10, local copies, waits for them, and re-layouts  5.19 us

profile of v4, /device:TPU:1, one launch (start us, length us, event | category | flops | bytes accessed | tf_op | source)
XLA Modules:
  0.0 191.5 jit_solution(11982475824875875118)
XLA Ops:
  0.6 185.6 %linear_attention.1 = (bf16[128,2048]{1,0:T(8,128)(2,1)}, bf16[128,2048]{1,0:T(8,128)(2,1)}, bf16[128,2048]{1,0:T(8,128)(2,1)}, bf16[128,2048]{1,0:T(8,128)(2,1)}) custom-call(bf16[128,2048]{1,0:T(8,128)(2,1)} %q_ref.1, bf16[128,2048]{1,0:T(8,128)(2,1)} %k_ref.1, bf16[128,2048]{1,0:T(8,128)(2,1)} %v_ref.1, bf16[128,2048]{1,0:T(8,128)(2,1)} %g_ref.1), custom_call_target="tpu_custom_call" | custom-call | tf_op jit(solution)/shard_map/linear_attention/pallas_call | solution.py:398
  186.3 0.0 copy-start.2
  186.3 1.9 %copy.12 = bf16[128,2048]{1,0:T(8,128)(2,1)} copy(bf16[128,2048]{1,0:T(8,128)(2,1)} %get-tuple-element.8) | data formatting | bytes 1048576
  188.2 0.0 copy-done.2
  188.2 0.0 copy-start.1
  188.2 0.8 copy.13
  189.0 0.4 copy-done.1
  189.5 0.0 copy-start
  189.5 0.8 copy.14
  190.3 0.4 copy-done
  190.7 0.8 copy.15
Async XLA Ops:
  186.3 2.0 %copy-start.2 = (bf16[128,2048]{1,0:T(8,128)(2,1)S(1)}, bf16[128,2048]{1,0:T(8,128)(2,1)}, u32[]{:S(2)}) copy-start(bf16[128,2048]{1,0:T(8,128)(2,1)} %get-tuple-element.9) | copy-start | bytes 1572868
  188.2 1.2 copy-start.1
  189.5 1.2 copy-start
